TPU v7x, 256 devices: a whole 4x4x8 slice. The times are simulated.
256 devices in a mesh: dp: 8 (over y, z_lo), fsdp: 32 (over z_hi, x, core).
Axes of the slice: x: 4, y: 4, z: 8 (z_hi: 4, z_lo: 2; z = z_hi * 2 + z_lo), core: 2. Of those that a mesh axis runs over, the one named last changes fastest.
Arguments:
- acts: bfloat16 [114688, 7168], P(('dp', 'fsdp')), may hold values from -24 to 24
- upstream: bfloat16 [114688, 512], P(('dp', 'fsdp')), may hold values from -0.4375 to 0.4375
- k_weight: bfloat16 [7168, 512], P('fsdp'), may hold values from -0.0625 to 0.0625
- probe: bfloat16 [7168, 512], P('fsdp'), may hold values from -5 to 5
- norm_gain: float32 [128], replicated, may hold values from 0.1 to 1.9
- momentum: float32 [7168, 512], P('fsdp', 'dp'), may hold values from -4 to 4
- curvature: float32 [7168, 512], P('fsdp', 'dp'), may hold values from 0.3 to 3
Outputs:
- new_momentum: float32 [7168, 512], P('fsdp', 'dp')
- new_curvature: float32 [7168, 512], P('fsdp', 'dp')
- update: float32 [7168, 512], P('fsdp', 'dp')
All inputs are finite; a program needn't handle non-finite values.
Results may differ from a plain program's by a relative error of at most 0.024.
Values may be sent and summed in bfloat16 or wider, within the bound.
A program may use at most 128 MiB of HBM per device.

v0:
```python
import jax
import jax.numpy as jnp
from jax import lax
from jax.sharding import PartitionSpec as P


def head_terms(projected, tangent, upstream, norm_gain):
    token_count = projected.shape[0]
    head_size = norm_gain.shape[0]
    head_count = projected.shape[1] // head_size
    shaped = (token_count, head_count, head_size)
    values = projected.reshape(shaped)
    moving = tangent.reshape(shaped)
    weighted = upstream.astype(jnp.float32).reshape(shaped) * norm_gain
    inverse = lax.rsqrt(jnp.mean(values * values, axis=-1, keepdims=True) + 1e-06)
    cubed = inverse * inverse * inverse
    along = jnp.sum(weighted * values, axis=-1, keepdims=True)
    grad_vals = inverse * weighted - cubed * values * along / head_size
    inverse_dot = -cubed * jnp.sum(values * moving, axis=-1, keepdims=True) / head_size
    along_dot = jnp.sum(weighted * moving, axis=-1, keepdims=True)
    hvp_vals = (
        inverse_dot * weighted
        - (
            3.0 * inverse * inverse * inverse_dot * values * along
            + cubed * moving * along
            + cubed * values * along_dot
        )
        / head_size
    )
    return (grad_vals.reshape(token_count, -1), hvp_vals.reshape(token_count, -1))


def contract_tokens(left, right):
    return lax.dot_general(
        left, right, (((0,), (0,)), ((), ())), preferred_element_type=jnp.float32
    )


def on_device(acts, upstream, k_weight, probe, norm_gain, momentum, curvature):
    width = k_weight.shape[1]
    weight_piece = lax.all_gather(k_weight, "fsdp", axis=0, tiled=True)
    probe_piece = lax.all_gather(probe, "fsdp", axis=0, tiled=True)
    projected = jnp.dot(acts, weight_piece, preferred_element_type=jnp.float32)
    tangent = jnp.dot(acts, probe_piece, preferred_element_type=jnp.float32)
    grad_vals, hvp_vals = head_terms(projected, tangent, upstream, norm_gain)
    stacked = jnp.concatenate([grad_vals, hvp_vals], axis=1).astype(jnp.bfloat16)
    owned = lax.psum_scatter(
        contract_tokens(acts, stacked).astype(jnp.bfloat16), "fsdp", scatter_dimension=0, tiled=True
    ).astype(jnp.float32)
    grad_owned = owned[:, :width]
    hvp_owned = owned[:, width:]
    grad_share, hvp_share = (
        lax.psum_scatter(grad_owned, "dp", scatter_dimension=1, tiled=True),
        lax.psum_scatter(hvp_owned, "dp", scatter_dimension=1, tiled=True),
    )
    share_width = grad_share.shape[1]
    probe_cols = lax.dynamic_slice_in_dim(
        probe, lax.axis_index("dp") * share_width, share_width, 1
    ).astype(jnp.float32)
    new_momentum = 0.965 * momentum + 0.035 * grad_share
    new_curvature = 0.99 * curvature + 0.01 * (probe_cols * hvp_share)
    update = jnp.clip(new_momentum / jnp.maximum(0.5 * new_curvature, 0.25), -1.0, 1.0)
    return (new_momentum, new_curvature, update)


def solution(mesh):
    return jax.shard_map(
        on_device,
        mesh=mesh,
        in_specs=(
            P(("dp", "fsdp"), None),
            P(("dp", "fsdp"), None),
            P("fsdp", None),
            P("fsdp", None),
            P(),
            P("fsdp", "dp"),
            P("fsdp", "dp"),
        ),
        out_specs=(P("fsdp", "dp"), P("fsdp", "dp"), P("fsdp", "dp")),
        check_vma=False,
    )
```

profile of v0, /device:TPU:2, one launch (start us, length us, event | category | flops | bytes accessed | tf_op | source)
XLA Modules:
  0.0 465.9 jit_solution(4802881140647189085)
XLA Ops:
  7.2 0.0 all-gather.3.cloned.1.call-start
  7.2 0.7 all-gather.3.cloned.1.call-update
  7.9 0.0 all-gather.5.cloned.1.call-start
  7.9 0.7 all-gather.5.cloned.1.call-update
  8.6 0.0 reduce-scatter.10.cloned.1.call-start
  8.7 1.3 reshape.67
  10.0 0.7 broadcast_bitcast_fusion
  10.7 75.3 %all-gather.3.cloned.1.call-done = bf16[7168,512]{1,0:T(8,128)(2,1)} async-done(((bf16[224,512]{1,0:T(8,128)(2,1)}), bf16[7168,512]{1,0:T(8,128)(2,1)}) %all-gather.3.cloned.1.call-update) | async-done | bytes 7340048 | tf_op jit(solution)/shard_map/all_gather | solution.py:41
  86.0 7.7 %fusion.23 = f32[448,512]{1,0:T(8,128)S(1)} fusion(bf16[448,7168]{1,0:T(8,128)(2,1)} %param.7, bf16[7168,512]{1,0:T(8,128)(2,1)} %all-gather.3.cloned.1.call-done), kind=kOutput, calls=%fused_computation.44 | convolution fusion | flops 3288334336 | bytes 14680064 | tf_op jit(solution)/shard_map/dot_general | solution.py:43
  93.7 0.3 reshape.66
  94.0 0.0 copy-start.7
  94.0 66.8 %all-gather.5.cloned.1.call-done = bf16[7168,512]{1,0:T(8,128)(2,1)} async-done(((bf16[224,512]{1,0:T(8,128)(2,1)}), bf16[7168,512]{1,0:T(8,128)(2,1)}) %all-gather.5.cloned.1.call-update) | async-done | bytes 7340048 | tf_op jit(solution)/shard_map/all_gather | solution.py:42
  160.8 9.4 %fusion.24 = f32[448,512]{1,0:T(8,128)} fusion(bf16[448,7168]{1,0:T(8,128)(2,1)} %param.7, bf16[7168,512]{1,0:T(8,128)(2,1)} %all-gather.5.cloned.1.call-done), kind=kOutput, calls=%fused_computation.45 | convolution fusion | flops 3288334336 | bytes 14680064 | tf_op jit(solution)/shard_map/dot_general | solution.py:44
  170.2 1.5 reshape.68
  171.7 0.0 copy-start.4
  171.7 1.6 multiply_reduce_fusion.3
  173.3 1.5 fusion
  174.9 1.5 fusion.1
  176.3 1.2 copy.17
  177.5 0.1 copy.20
  177.7 0.1 copy.22
  177.8 0.9 copy.18
  178.7 0.8 copy.19
  179.5 0.8 copy.21
  180.3 0.5 mul.254
  180.9 1.7 mul.227
  182.6 1.5 mul.236
  184.1 1.5 mul.247
  185.6 0.0 copy-done.4
  185.6 0.0 copy-done.1
  185.6 0.0 copy-done.2
  185.6 0.0 slice-start.1
  185.6 2.3 fusion.10
  188.0 11.3 %convert_bitcast_fusion = bf16[7168,1024]{0,1:T(8,128)(2,1)} fusion(bf16[448,7168]{1,0:T(8,128)(2,1)S(1)} %bitcast.67, bf16[448,512]{1,0:T(8,128)(2,1)S(1)} %get-tuple-element.9, bf16[448,512]{1,0:T(8,128)(2,1)S(1)} %get-tuple-element.8), kind=kOutput, calls=%fused_computation.2 | convolution fusion | flops 6585843712 | bytes 22020096 | tf_op jit(solution)/shard_map/dot_general | solution.py:34
  199.3 19.9 %copy.24 = bf16[7168,1024]{1,0:T(8,128)(2,1)} copy(bf16[7168,1024]{0,1:T(8,128)(2,1)} %convert_bitcast_fusion) | data formatting | bytes 29360128
  219.2 0.0 reduce-scatter.10.cloned.1.call-update
  219.2 0.0 reduce-scatter.6.cloned.1.call-start
  219.3 154.1 %reduce-scatter.10.cloned.1.call-done = bf16[224,1024]{1,0:T(8,128)(2,1)} async-done(((bf16[7168,1024]{1,0:T(8,128)(2,1)}), bf16[224,1024]{1,0:T(8,128)(2,1)}) %reduce-scatter.10.cloned.1.call-update) | async-done | bytes 458768
  373.3 1.2 copy.25
  374.6 1.0 fusion.22
  375.6 0.0 reduce-scatter.6.cloned.1.call-update
  375.6 0.0 reduce-scatter.8.cloned.1.call-start
  375.7 0.5 reduce-scatter.8.cloned.1.call-update
  376.2 0.9 constant_dynamic-slice_fusion
  377.1 0.1 copy.26
  377.2 38.8 %reduce-scatter.6.cloned.1.call-done = f32[224,64]{0,1:T(8,128)} async-done(((f32[224,512]{0,1:T(8,128)}), f32[224,64]{0,1:T(8,128)}) %reduce-scatter.6.cloned.1.call-update) | async-done | bytes 57360 | tf_op jit(solution)/shard_map/reduce_scatter | solution.py:53
  416.0 41.8 %reduce-scatter.8.cloned.1.call-done = f32[224,64]{0,1:T(8,128)} async-done(((f32[224,512]{0,1:T(8,128)}), f32[224,64]{0,1:T(8,128)}) %reduce-scatter.8.cloned.1.call-update) | async-done | bytes 57360 | tf_op jit(solution)/shard_map/reduce_scatter | solution.py:54
  457.8 1.6 divide_clamp_fusion
  (16 shorter events, 0.1 us)
Async XLA Ops:
  7.2 78.8 %all-gather.3.cloned.1.call-start = ((), (), s32[]{:S(2)}) async-start(), calls=%async_computation.3 | async-start | bytes 7569408 | tf_op jit(solution)/shard_map/all_gather | solution.py:41
  7.9 152.9 %all-gather.5.cloned.1.call-start = ((), (), s32[]{:S(2)}) async-start(), calls=%async_computation.4 | async-start | bytes 7569408 | tf_op jit(solution)/shard_map/all_gather | solution.py:42
  8.6 364.7 %reduce-scatter.10.cloned.1.call-start = ((), (), s32[]{:S(2)}) async-start(), calls=%async_computation.7 | async-start | bytes 15138816
  93.7 67.1 %copy-start = (f32[448,512]{1,0:T(8,128)}, f32[448,512]{1,0:T(8,128)S(1)}, u32[]{:S(2)}) copy-start(f32[448,512]{1,0:T(8,128)S(1)} %fusion.23) | copy-start | bytes 2752516
  94.0 79.3 %copy-start.7 = (f32[128]{0:T(128)S(1)}, f32[128]{0:T(128)}, u32[]{:S(2)}) copy-start(f32[128]{0:T(128)} %param.11) | copy-start | bytes 1540
  171.7 13.9 %copy-start.4 = (bf16[448,512]{1,0:T(8,128)(2,1)S(1)}, bf16[448,512]{1,0:T(8,128)(2,1)}, u32[]{:S(2)}) copy-start(bf16[448,512]{1,0:T(8,128)(2,1)} %param.8) | copy-start | bytes 1376260
  174.9 10.7 %copy-start.1 = (f32[448,512]{1,0:T(8,128)S(1)}, f32[448,512]{1,0:T(8,128)}, u32[]{:S(2)}) copy-start(f32[448,512]{1,0:T(8,128)} %copy-done) | copy-start | bytes 2752516
  176.3 9.3 %copy-start.2 = (f32[448,512]{1,0:T(8,128)S(1)}, f32[448,512]{1,0:T(8,128)}, u32[]{:S(2)}) copy-start(f32[448,512]{1,0:T(8,128)} %fusion.24) | copy-start | bytes 2752516
  176.3 9.3 %copy-start.3 = (f32[448,4,128]{2,1,0:T(4,128)S(1)}, f32[448,4,128]{2,1,0:T(4,128)}, u32[]{:S(2)}) copy-start(f32[448,4,128]{2,1,0:T(4,128)} %fusion) | copy-start | bytes 2752516
  180.3 7.6 %slice-start = ((s8[6422528]{0:T(1024)(128)(4,1)}), s8[4194304]{0:T(1024)(128)(4,1)S(1)}, s32[]{:S(2)}) async-start(s8[6422528]{0:T(1024)(128)(4,1)} %bitcast.66), calls=%async_computation.8 | async-start | bytes 8388608
  185.6 2.3 slice-start.1
  219.2 238.6 %copy-start.5 = (f32[224,64]{0,1:T(8,128)S(1)}, f32[224,64]{0,1:T(8,128)}, u32[]{:S(2)}) copy-start(f32[224,64]{0,1:T(8,128)} %param.13) | copy-start | bytes 172036
  219.2 238.6 %copy-start.6 = (f32[224,64]{0,1:T(8,128)S(1)}, f32[224,64]{0,1:T(8,128)}, u32[]{:S(2)}) copy-start(f32[224,64]{0,1:T(8,128)} %param.12) | copy-start | bytes 172036
  219.2 196.8 %reduce-scatter.6.cloned.1.call-start = ((), (), s32[]{:S(2)}) async-start(), calls=%async_computation.5 | async-start | bytes 589824 | tf_op jit(solution)/shard_map/reduce_scatter | solution.py:53
  375.6 82.2 %reduce-scatter.8.cloned.1.call-start = ((), (), s32[]{:S(2)}) async-start(), calls=%async_computation.6 | async-start | bytes 589824 | tf_op jit(solution)/shard_map/reduce_scatter | solution.py:54
Sparse Core Ops, SparseCore 0:
  10.5 75.4 all-gather.2
  88.5 72.2 all-gather.4
  219.3 153.9 reduce-scatter.9
  375.8 40.2 reduce-scatter.5
  418.4 39.4 reduce-scatter.7
where the time goes:
time: 467 us; the launch traced here: 466 us
  waiting for transfers between devices  379 us (81%)
  local copies, waits for them, and re-layouts  36.1 us (8%)
  matrix products  28.4 us (6%)
  between operations  13.9 us (3%)
  other arithmetic  8.53 us (2%)
    unnamed x6, waiting for transfers between devices  156 us
    all_gather x1, waiting for transfers between devices, on_device(): weight_piece = lax.all_gather(k_weight, 'fsdp', axis=0, tiled=True)  75.3 us
    all_gather x1, waiting for transfers between devices, on_device(): probe_piece = lax.all_gather(probe, 'fsdp', axis=0, tiled=True)  66.8 us
    reduce_scatter x1, waiting for transfers between devices, on_device(): lax.psum_scatter(hvp_owned, 'dp', scatter_dimension=1, tiled=True)  41.8 us
    reduce_scatter x1, waiting for transfers between devices, on_device(): lax.psum_scatter(grad_owned, 'dp', scatter_dimension=1, tiled=True)  38.8 us
    unnamed x23, local copies, waits for them, and re-layouts  21.3 us
    dot_general x1, matrix products, contract_tokens(): lax.dot_general(left, right, (((0,), (0,)), ((), ())), preferred_element_...  11.3 us
    dot_general x1, matrix products, on_device(): tangent = jnp.dot(acts, probe_piece, preferred_element_type=jnp.float32)  9.36 us
  transfers between devices with their start and end apart: 5, of which 5 were waited for; matrix products, arithmetic and copies ran while one was open for 2% of the time, Pallas kernels for 0%

commit v1 on v0

--- a/solution.py
+++ b/solution.py
@@ -38,7 +38,12 @@
 
 def on_device(acts, upstream, k_weight, probe, norm_gain, momentum, curvature):
     width = k_weight.shape[1]
-    weight_piece = lax.all_gather(k_weight, "fsdp", axis=0, tiled=True)
+    weight_piece = jnp.concatenate(
+        lax.all_to_all(
+            jnp.stack(tuple((k_weight for _ in range(lax.axis_size("fsdp")))), axis=0), "fsdp", 0, 0
+        ),
+        0,
+    )
     probe_piece = lax.all_gather(probe, "fsdp", axis=0, tiled=True)
     projected = jnp.dot(acts, weight_piece, preferred_element_type=jnp.float32)
     tangent = jnp.dot(acts, probe_piece, preferred_element_type=jnp.float32)

time: 467 us -> 529 us (1.13)
  waiting for transfers between devices: 379 us -> 432 us
  starting transfers between devices: 0.2 us -> 11.8 us
    all_to_all x0 -> x1, waiting for transfers between devices: none -> 199 us  [on_device(): lax.all_to_all(jnp.stack(tuple((k_weight for _ in range(lax.axis_size('fs...]
    all_gather x1 -> x0, waiting for transfers between devices: 75.3 us -> none  [on_device(): weight_piece = lax.all_gather(k_weight, 'fsdp', axis=0, tiled=True)]
    all_gather x1, waiting for transfers between devices: 66.8 us -> 0.01 us  [on_device(): probe_piece = lax.all_gather(probe, 'fsdp', axis=0, tiled=True)]
    all_to_all x0 -> x1, starting transfers between devices: none -> 11.7 us  [on_device(): lax.all_to_all(jnp.stack(tuple((k_weight for _ in range(lax.axis_size('fs...]
    dot_general x0 -> x1, local copies, waits for them, and re-layouts: none -> 9.98 us  [on_device(): projected = jnp.dot(acts, weight_piece, preferred_element_type=jnp.float32)]
    mul x7 -> x0, local copies, waits for them, and re-layouts: 6.84 us -> none  [the longest x2 3.21 us: head_terms(): grad_vals = inverse * weighted - cubed * values * along / head_size]
    unnamed x6 -> x5, waiting for transfers between devices: 156 us -> 152 us
    unnamed x23 -> x17, local copies, waits for them, and re-layouts: 21.3 us -> 21.2 us
  transfers between devices with their start and end apart: 5 -> 5, of which waited for: 5 -> 4; matrix products, arithmetic and copies ran while one was open for 2% -> 2% of each run, Pallas kernels for 0% -> 0%
where the time goes in v1:
time: 529 us; the launch traced here: 528 us
  waiting for transfers between devices  432 us (82%)
  local copies, waits for them, and re-layouts  37.9 us (7%)
  matrix products  26.2 us (5%)
  between operations  13.9 us (3%)
  starting transfers between devices  11.8 us (2%)
  other arithmetic  5.9 us (1%)
    all_to_all x1, waiting for transfers between devices, on_device(): lax.all_to_all(jnp.stack(tuple((k_weight for _ in range(lax.axis_size('fs...  199 us
    unnamed x5, waiting for transfers between devices  152 us
    reduce_scatter x1, waiting for transfers between devices, on_device(): lax.psum_scatter(hvp_owned, 'dp', scatter_dimension=1, tiled=True)  41.7 us
    reduce_scatter x1, waiting for transfers between devices, on_device(): lax.psum_scatter(grad_owned, 'dp', scatter_dimension=1, tiled=True)  39.2 us
    unnamed x17, local copies, waits for them, and re-layouts  21.2 us
    all_to_all x1, starting transfers between devices, on_device(): lax.all_to_all(jnp.stack(tuple((k_weight for _ in range(lax.axis_size('fs...  11.7 us
    dot_general x1, matrix products, contract_tokens(): lax.dot_general(left, right, (((0,), (0,)), ((), ())), preferred_element_...  11.1 us
  transfers between devices with their start and end apart: 5, of which 4 were waited for; matrix products, arithmetic and copies ran while one was open for 2% of the time, Pallas kernels for 0%

profile of v1, /device:TPU:2, one launch (start us, length us, event | category | flops | bytes accessed | tf_op | source)
XLA Modules:
  0.0 528.1 jit_solution(8030077217894572399)
XLA Ops:
  7.2 4.7 stack.2
  11.9 11.7 %all-to-all-start = ((bf16[32,224,512]{2,1,0:T(8,128)(2,1)}), bf16[32,224,512]{2,1,0:T(8,128)(2,1)}, u32[]{:S(2)}, u32[]{:S(2)}) async-start(bf16[32,224,512]{2,1,0:T(8,128)(2,1)} %stack.2), calls=%async_computation | async-start | bytes 14680064 | tf_op jit(solution)/shard_map/all_to_all | solution.py:42
  23.5 0.0 all-gather.2.cloned.1.call-start
  23.6 0.7 all-gather.2.cloned.1.call-update
  24.3 0.0 reduce-scatter.10.cloned.1.call-start
  24.3 199.5 %all-to-all-done = bf16[32,224,512]{2,1,0:T(8,128)(2,1)} async-done(((bf16[32,224,512]{2,1,0:T(8,128)(2,1)}), bf16[32,224,512]{2,1,0:T(8,128)(2,1)}, u32[]{:S(2)}, u32[]{:S(2)}) %all-to-all-start) | async-done | bytes 7340064 | tf_op jit(solution)/shard_map/all_to_all | solution.py:42
  223.8 10.0 %copy.20 = bf16[512,7168]{1,0:T(8,128)(2,1)} copy(bf16[512,7168]{0,1:T(8,128)(2,1)} %bitcast.2) | data formatting | bytes 14680064 | tf_op jit(solution)/shard_map/dot_general | solution.py:48
  233.8 0.0 copy-start.1
  233.8 0.0 copy-start.4
  233.8 0.0 all-gather.2.cloned.1.call-done
  233.8 0.0 copy-start
  233.8 0.0 slice-start
  233.8 7.8 %convolution_bitcast_fusion = f32[56,4,8,128]{3,2,1,0:T(8,128)S(1)} fusion(bf16[448,7168]{1,0:T(8,128)(2,1)} %param.7, bf16[7168,512]{1,0:T(8,128)(2,1)} %all-gather.2.cloned.1.call-done), kind=kOutput, calls=%fused_computation.8 | convolution fusion | flops 3288334336 | bytes 14680064 | tf_op jit(solution)/shard_map/dot_general | solution.py:49
  241.6 0.0 copy-done.1
  241.6 0.0 copy-done.4
  241.7 0.0 copy-done
  241.7 0.0 slice-start.1
  241.7 7.3 %multiply_reduce_fusion = (f32[448,4]{0,1:T(4,128)S(1)}, f32[448,4]{0,1:T(4,128)S(1)}, f32[448,4]{0,1:T(4,128)S(1)}, f32[448,4,128]{2,0,1:T(8,128)S(1)}) fusion(f32[128]{0:T(128)S(1)} %copy-done.4, f32[56,4,8,128]{3,2,1,0:T(8,128)S(1)} %convolution_bitcast_fusion, bf16[4,128,7168]{2,1,0:T(8,128)(2,1)S(1)} %bitcast.66, bf16[448,7168]{1,0:T(8,128)(2,1)} %param.7, ...), kind=kOutput, calls=%fused_computation.23 | convolution fusion | flops 3290163968 | bytes 16078336 | tf_op jit(solution)/shard_map/dot_general | solution.py:48
  249.0 3.3 fusion.8
  252.3 1.0 copy_bitcast_fusion
  253.3 0.0 slice-done
  253.3 0.0 slice-done.1
  253.4 11.1 %convert_bitcast_fusion = bf16[7168,1024]{0,1:T(8,128)(2,1)} fusion(bf16[448,7168]{1,0:T(8,128)(2,1)S(1)} %bitcast.68, bf16[448,512]{1,0:T(8,128)(2,1)S(1)} %get-tuple-element.18, bf16[448,512]{1,0:T(8,128)(2,1)S(1)} %get-tuple-element.19), kind=kOutput, calls=%fused_computation.1 | convolution fusion | flops 6585843712 | bytes 22020096 | tf_op jit(solution)/shard_map/dot_general | solution.py:34
  264.4 19.9 %copy.28 = bf16[7168,1024]{1,0:T(8,128)(2,1)} copy(bf16[7168,1024]{0,1:T(8,128)(2,1)} %convert_bitcast_fusion) | data formatting | bytes 29360128
  284.3 0.0 copy-start.2
  284.3 0.0 copy-start.3
  284.3 0.0 reduce-scatter.10.cloned.1.call-update
  284.4 0.0 reduce-scatter.6.cloned.1.call-start
  284.4 150.8 %reduce-scatter.10.cloned.1.call-done = bf16[224,1024]{1,0:T(8,128)(2,1)} async-done(((bf16[7168,1024]{1,0:T(8,128)(2,1)}), bf16[224,1024]{1,0:T(8,128)(2,1)}) %reduce-scatter.10.cloned.1.call-update) | async-done | bytes 458768
  435.2 1.2 copy.29
  436.5 1.0 fusion.20
  437.5 0.0 reduce-scatter.6.cloned.1.call-update
  437.5 0.0 reduce-scatter.8.cloned.1.call-start
  437.6 0.5 reduce-scatter.8.cloned.1.call-update
  438.1 0.9 constant_dynamic-slice_fusion
  439.0 0.1 copy.30
  439.1 39.2 %reduce-scatter.6.cloned.1.call-done = f32[224,64]{0,1:T(8,128)} async-done(((f32[224,512]{0,1:T(8,128)}), f32[224,64]{0,1:T(8,128)}) %reduce-scatter.6.cloned.1.call-update) | async-done | bytes 57360 | tf_op jit(solution)/shard_map/reduce_scatter | solution.py:58
  478.3 41.7 %reduce-scatter.8.cloned.1.call-done = f32[224,64]{0,1:T(8,128)} async-done(((f32[224,512]{0,1:T(8,128)}), f32[224,64]{0,1:T(8,128)}) %reduce-scatter.8.cloned.1.call-update) | async-done | bytes 57360 | tf_op jit(solution)/shard_map/reduce_scatter | solution.py:59
  520.0 0.0 copy-done.2
  520.0 0.0 copy-done.3
  520.0 1.6 divide_clamp_fusion
  (2 shorter events, 0.0 us)
Async XLA Ops:
  11.9 211.9 %all-to-all-start = ((bf16[32,224,512]{2,1,0:T(8,128)(2,1)}), bf16[32,224,512]{2,1,0:T(8,128)(2,1)}, u32[]{:S(2)}, u32[]{:S(2)}) async-start(bf16[32,224,512]{2,1,0:T(8,128)(2,1)} %stack.2), calls=%async_computation | async-start | bytes 14680064 | tf_op jit(solution)/shard_map/all_to_all | solution.py:42
  23.5 210.2 %all-gather.2.cloned.1.call-start = ((), (), s32[]{:S(2)}) async-start(), calls=%async_computation.4 | async-start | bytes 7569408 | tf_op jit(solution)/shard_map/all_gather | solution.py:47
  24.3 411.0 %reduce-scatter.10.cloned.1.call-start = ((), (), s32[]{:S(2)}) async-start(), calls=%async_computation.7 | async-start | bytes 15138816
  233.8 7.9 %copy-start.1 = (bf16[448,512]{1,0:T(8,128)(2,1)S(1)}, bf16[448,512]{1,0:T(8,128)(2,1)}, u32[]{:S(2)}) copy-start(bf16[448,512]{1,0:T(8,128)(2,1)} %param.8) | copy-start | bytes 1376260
  233.8 7.9 %copy-start.4 = (f32[128]{0:T(128)S(1)}, f32[128]{0:T(128)}, u32[]{:S(2)}) copy-start(f32[128]{0:T(128)} %param.11) | copy-start | bytes 1540
  233.8 7.9 %copy-start = (bf16[512,7168]{1,0:T(8,128)(2,1)S(1)}, bf16[512,7168]{1,0:T(8,128)(2,1)}, u32[]{:S(2)}) copy-start(bf16[512,7168]{1,0:T(8,128)(2,1)} %copy.20) | copy-start | bytes 22020100
  233.8 19.5 %slice-start = ((s8[6422528]{0:T(1024)(128)(4,1)}), s8[4194304]{0:T(1024)(128)(4,1)S(1)}, s32[]{:S(2)}) async-start(s8[6422528]{0:T(1024)(128)(4,1)} %bitcast.67), calls=%async_computation.8 | async-start | bytes 8388608
  241.7 11.7 %slice-start.1 = ((s8[6422528]{0:T(1024)(128)(4,1)}), s8[2228224]{0:T(1024)(128)(4,1)S(1)}, s32[]{:S(2)}) async-start(s8[6422528]{0:T(1024)(128)(4,1)} %bitcast.67), calls=%async_computation.9 | async-start | bytes 4456448
  284.3 235.7 %copy-start.2 = (f32[224,64]{0,1:T(8,128)S(1)}, f32[224,64]{0,1:T(8,128)}, u32[]{:S(2)}) copy-start(f32[224,64]{0,1:T(8,128)} %param.13) | copy-start | bytes 172036
  284.3 235.7 %copy-start.3 = (f32[224,64]{0,1:T(8,128)S(1)}, f32[224,64]{0,1:T(8,128)}, u32[]{:S(2)}) copy-start(f32[224,64]{0,1:T(8,128)} %param.12) | copy-start | bytes 172036
  284.4 193.9 %reduce-scatter.6.cloned.1.call-start = ((), (), s32[]{:S(2)}) async-start(), calls=%async_computation.5 | async-start | bytes 589824 | tf_op jit(solution)/shard_map/reduce_scatter | solution.py:58
  437.5 82.5 %reduce-scatter.8.cloned.1.call-start = ((), (), s32[]{:S(2)}) async-start(), calls=%async_computation.6 | async-start | bytes 589824 | tf_op jit(solution)/shard_map/reduce_scatter | solution.py:59
Sparse Core Ops, SparseCore 0:
  26.9 181.2 all-gather.1
  284.5 150.6 reduce-scatter.9
  437.8 40.4 reduce-scatter.5
  480.6 39.3 reduce-scatter.7
